TPU v7x, 256 devices: a whole 4x4x8 slice. The times are simulated.
256 devices in a mesh: member: 32 (over x, y, core), grid: 8 (over z).
Axes of the slice: x: 4, y: 4, z: 8, core: 2. Of those that a mesh axis runs over, the one named last changes fastest.
Arguments:
- prior_ensemble: bfloat16 [512, 48, 32768], P('member', None, 'grid'), may hold values from -6 to 6
- measured_location: int32 [8, 32, 128], P('grid', 'member'), may hold values from 0 to 6143
- measured_tally: int32 [8, 32], P('grid', 'member'), may hold values from 32 to 128, as said below
- measured_reading: float32 [8, 32, 128], P('grid', 'member'), may hold values from -6 to 6
- measured_noise_sigma: float32 [8, 32, 128], P('grid', 'member'), may hold values from 0.5 to 20, as said below
Outputs:
- analysis: bfloat16 [512, 48, 32768], P('member', None, 'grid')
Inputs may be any that keep to these rules, and one draw needn't show every extreme that they name: `measured_location`: cell of the observation within its block of 48 rows and 128 columns. `measured_tally`: some block in every draw uses all 128 slots. `measured_noise_sigma`: positive error deviations.
All inputs are finite; a program needn't handle non-finite values.
Results may differ from a plain program's by a relative error of at most 0.0058.
Values may be sent and summed in bfloat16 or wider, within the bound.
A program may use at most 128 MiB of HBM per device.

v0:
```python
import jax
import jax.numpy as jnp
from jax import lax
from jax.sharding import PartitionSpec as P

HIGHEST_PRECISION = lax.Precision.HIGHEST


def whiten(hx_values, values, errors, obs_total):
    hx_float = hx_values.astype(jnp.float32)
    hx_mean = jnp.mean(hx_float, axis=0)
    usable = (jnp.arange(hx_values.shape[1], dtype=jnp.int32) < obs_total).astype(jnp.float32)
    scale_obs = usable / errors
    whitened = (hx_float - hx_mean) * scale_obs
    innovation = (values - hx_mean) * scale_obs
    return (whitened, innovation)


def transform_matrix(gram_total, drive_vector):
    members = gram_total.shape[0]
    identity = jnp.eye(members, dtype=jnp.float32)
    system = (members - 1.0) * identity + gram_total
    factor_low = jnp.linalg.cholesky(system)
    inverse = jax.scipy.linalg.solve_triangular(factor_low, identity, lower=True)
    inner = jnp.dot(inverse, drive_vector, precision=HIGHEST_PRECISION)
    mean_weight = jnp.dot(inverse.T, inner, precision=HIGHEST_PRECISION)
    spread = jnp.sqrt(members - 1.0) * inverse.T
    return (mean_weight[:, None] + spread).astype(jnp.bfloat16)


def local_sums(whitened, innovation):
    gram_local = lax.dot_general(
        whitened, whitened, (((1,), (1,)), ((), ())), precision=HIGHEST_PRECISION
    )
    drive_local = jnp.dot(whitened, innovation, precision=HIGHEST_PRECISION)
    return (gram_local, drive_local)


def reduce_gram(whitened, innovation):
    gram_local, drive_local = local_sums(whitened, innovation)
    gram_total, drive_vector = lax.psum((gram_local, drive_local), ("member", "grid"))
    return transform_matrix(gram_total, drive_vector)


def apply_block(state_block, transform):
    members, row_count, columns = state_block.shape
    flattened = state_block.reshape(members, row_count * columns)
    state_mean = jnp.mean(flattened.astype(jnp.float32), axis=0)
    anomalies = (flattened.astype(jnp.float32) - state_mean).astype(jnp.bfloat16)
    increment = lax.dot_general(
        transform, anomalies, (((0,), (0,)), ((), ())), preferred_element_type=jnp.float32
    )
    return (state_mean + increment).astype(jnp.bfloat16).reshape(members, row_count, columns)


def local(
    prior_ensemble, measured_location, measured_tally, measured_reading, measured_noise_sigma
):
    values = measured_reading[0, 0]
    errors = measured_noise_sigma[0, 0]
    obs_total = measured_tally[0, 0]
    shard_profiles = lax.all_to_all(
        prior_ensemble, "member", split_axis=2, concat_axis=0, tiled=True
    )
    members, row_count, columns = shard_profiles.shape
    hx_values = jnp.take(
        shard_profiles.reshape(members, row_count * columns), measured_location[0, 0], axis=1
    )
    whitened, innovation = whiten(hx_values, values, errors, obs_total)
    transform = reduce_gram(whitened, innovation)
    updated = apply_block(shard_profiles, transform)
    return lax.all_to_all(updated, "member", split_axis=0, concat_axis=2, tiled=True)


def solution(mesh):
    in_specs = (
        P("member", None, "grid"),
        P("grid", "member", None),
        P("grid", "member"),
        P("grid", "member", None),
        P("grid", "member", None),
    )
    out_specs = P("member", None, "grid")
    return jax.shard_map(local, mesh=mesh, in_specs=in_specs, out_specs=out_specs, check_vma=False)
```

profile of v0, /device:TPU:1, one launch (start us, length us, event | category | flops | bytes accessed | tf_op | source)
XLA Modules:
  0.0 763.0 jit_solution(7519993507879228197)
XLA Ops:
  6.5 19.4 %copy.19 = bf16[16,48,4096]{1,0,2:T(8,128)(2,1)} copy(bf16[16,48,4096]{2,1,0:T(8,128)(2,1)} %param.5) | data formatting | bytes 12582912 | tf_op args[0]
  25.9 31.8 %reshape.139 = bf16[32,2,49152]{2,1,0:T(2,128)(2,1)} reshape(bf16[4096,16,48]{2,1,0:T(8,128)(2,1)} %bitcast.111) | data formatting | bytes 12582912
  57.7 8.8 %all-to-all-start = ((bf16[32,2,49152]{2,1,0:T(2,128)(2,1)}), bf16[32,2,49152]{2,1,0:T(2,128)(2,1)}, u32[]{:S(2)}, u32[]{:S(2)}) async-start(bf16[32,2,49152]{2,1,0:T(2,128)(2,1)} %reshape.139), calls=%async_computation | async-start | bytes 12582912 | tf_op jit(solution)/shard_map/all_to_all | solution.py:62
  68.9 74.8 %all-to-all-done = bf16[32,2,49152]{2,1,0:T(2,128)(2,1)} async-done(((bf16[32,2,49152]{2,1,0:T(2,128)(2,1)}), bf16[32,2,49152]{2,1,0:T(2,128)(2,1)}, u32[]{:S(2)}, u32[]{:S(2)}) %all-to-all-start) | async-done | bytes 6291488 | tf_op jit(solution)/shard_map/all_to_all | solution.py:62
  143.7 27.6 %reshape.140 = bf16[4096,16,48]{2,1,0:T(8,128)(2,1)} reshape(bf16[32,2,49152]{2,1,0:T(2,128)(2,1)} %all-to-all-done) | data formatting | bytes 12582912
  171.3 18.8 %copy.20 = bf16[16,48,32,128]{3,1,0,2:T(8,128)(2,1)} copy(bf16[16,48,32,128]{1,0,3,2:T(8,128)(2,1)} %bitcast.110) | data formatting | bytes 12582912 | tf_op jit(solution)/shard_map/all_to_all | solution.py:62
  190.1 7.1 copy.44
  197.1 8.7 %copy.21 = bf16[512,6144]{0,1:T(8,128)(2,1)} copy(bf16[512,6144]{1,0:T(8,128)(2,1)} %bitcast.119) | data formatting | bytes 12582912 | tf_op jit(solution)/shard_map/reshape | solution.py:47
  213.1 88.8 %psum.15 = f32[512]{0:T(512)S(1)} all-reduce(f32[512]{0:T(512)S(1)} %bitcast.121), channel_id=1, replica_groups=mesh['member'=32,'grid'=8] {'member','grid'}, use_global_device_ids=true, to_apply=%region_11.12 | all-reduce | flops 512 | bytes 4096 | tf_op jit(solution)/shard_map/psum | solution.py:41
  306.6 173.9 %all-reduce.3.cloned.1.call-done = f32[512,512]{0,1:T(8,128)} async-done(((f32[512,512]{0,1:T(8,128)}), f32[512,512]{0,1:T(8,128)}) %all-reduce.3.cloned.1.call-update) | async-done | bytes 1048592 | tf_op jit(solution)/shard_map/psum | solution.py:41
  483.6 11.7 %cholesky.107 = f32[128,128]{1,0:T(8,128)S(1)} custom-call(f32[128,128]{1,0:T(8,128)S(1)} %cholesky.269), custom_call_target="Cholesky" | custom-call | tf_op jit(solution)/shard_map/jit(cholesky)/cholesky | solution.py:23
  495.4 9.8 %custom-call.31 = f32[1,128,128]{1,2,0:T(8,128)S(1)} custom-call(f32[1,128,128]{2,1,0:T(8,128)S(1)} %get-tuple-element.36), custom_call_target="InvertDiagBlocksLowerTriangular" | custom-call | tf_op jit(solution)/shard_map/jit(cholesky)/cholesky | solution.py:23
  505.9 11.9 %cholesky.221 = f32[128,128]{1,0:T(8,128)S(1)} custom-call(f32[128,128]{1,0:T(8,128)S(1)} %cholesky.273), custom_call_target="Cholesky" | custom-call | tf_op jit(solution)/shard_map/jit(cholesky)/cholesky | solution.py:23
  518.1 9.8 %custom-call.32 = f32[1,128,128]{1,2,0:T(8,128)S(1)} custom-call(f32[1,128,128]{2,1,0:T(8,128)S(1)} %get-tuple-element.34), custom_call_target="InvertDiagBlocksLowerTriangular" | custom-call | tf_op jit(solution)/shard_map/jit(cholesky)/cholesky | solution.py:23
  530.7 13.2 %cholesky.242 = f32[128,128]{1,0:T(8,128)} custom-call(f32[128,128]{1,0:T(8,128)} %cholesky.278), custom_call_target="Cholesky" | custom-call | tf_op jit(solution)/shard_map/jit(cholesky)/cholesky | solution.py:23
  547.8 11.3 %custom-call.33 = f32[1,128,128]{1,2,0:T(8,128)} custom-call(f32[1,128,128]{2,1,0:T(8,128)} %get-tuple-element.32), custom_call_target="InvertDiagBlocksLowerTriangular" | custom-call | tf_op jit(solution)/shard_map/jit(cholesky)/cholesky | solution.py:23
  561.5 12.1 %cholesky.259 = f32[128,128]{1,0:T(8,128)S(1)} custom-call(f32[128,128]{1,0:T(8,128)S(1)} %convolution_subtract_fusion.5), custom_call_target="Cholesky" | custom-call | tf_op jit(solution)/shard_map/jit(cholesky)/cholesky | solution.py:23
  582.0 14.5 %while.1 = (s32[]{:T(128)}, f32[512,512]{0,1:T(8,128)}, s32[4,2]{0,1:T(2,128)S(1)}, f32[4,128,128]{2,1,0:T(8,128)}, s32[]{:T(128)}) while((s32[]{:T(128)}, f32[512,512]{0,1:T(8,128)}, s32[4,2]{0,1:T(2,128)S(1)}, f32[4,128,128]{2,1,0:T(8,128)}, s32[]{:T(128)}) %tuple.25), condition=%wide.while_cond, body=%wide.while_body.sunk | while | flops 2 | bytes 393829 | solution.py:24
  596.5 40.1 %custom-call.34 = f32[4,128,128]{1,2,0:T(8,128)S(1)} custom-call(f32[4,128,128]{2,1,0:T(8,128)} %get-tuple-element.12), custom_call_target="InvertDiagBlocksLowerTriangular" | custom-call | tf_op jit(solution)/shard_map/jit(_solve_triangular)/triangular_solve | solution.py:24
  646.3 6.7 fusion.1
  653.0 4.7 copy.38
  657.7 81.4 %all_to_all.33 = bf16[512,48,128]{2,1,0:T(8,128)(2,1)S(1)} all-to-all(bf16[512,48,128]{2,1,0:T(8,128)(2,1)S(1)} %bitcast.116), channel_id=1, replica_groups=mesh['member'=32,'grid'=8] {'member'}, dimensions={0} | all-to-all | bytes 12582912 | tf_op jit(solution)/shard_map/all_to_all | solution.py:72
  739.0 6.7 copy.45
  745.7 10.3 %all_to_all.30 = bf16[16,48,4096]{2,1,0:T(8,128)(2,1)} reshape(bf16[16,48,32,128]{3,2,1,0:T(8,128)(2,1)} %bitcast.118) | data formatting | bytes 12582912 | tf_op jit(solution)/shard_map/all_to_all | solution.py:72
  (92 shorter events, 56.9 us)
Async XLA Ops:
  57.6 10.1 %copy-start.3 = (s32[1,1,128]{2,1,0:T(1,128)S(1)}, s32[1,1,128]{2,1,0:T(1,128)}, u32[]{:S(2)}) copy-start(s32[1,1,128]{2,1,0:T(1,128)} %param.6) | copy-start | bytes 1540
  57.7 86.1 %all-to-all-start = ((bf16[32,2,49152]{2,1,0:T(2,128)(2,1)}), bf16[32,2,49152]{2,1,0:T(2,128)(2,1)}, u32[]{:S(2)}, u32[]{:S(2)}) async-start(bf16[32,2,49152]{2,1,0:T(2,128)(2,1)} %reshape.139), calls=%async_computation | async-start | bytes 12582912 | tf_op jit(solution)/shard_map/all_to_all | solution.py:62
  66.4 414.0 %all-reduce.3.cloned.1.call-start = ((), (), s32[]{:S(2)}) async-start(), calls=%async_computation.2 | async-start | bytes 2097152 | tf_op jit(solution)/shard_map/psum | solution.py:41
  197.1 13.3 %copy-start.2 = (f32[1,1,128]{2,1,0:T(1,128)S(1)}, f32[1,1,128]{2,1,0:T(1,128)}, u32[]{:S(2)}) copy-start(f32[1,1,128]{2,1,0:T(1,128)} %param.9) | copy-start | bytes 1540
  197.1 15.6 %copy-start.4 = (f32[1,1,128]{2,1,0:T(1,128)S(1)}, f32[1,1,128]{2,1,0:T(1,128)}, u32[]{:S(2)}) copy-start(f32[1,1,128]{2,1,0:T(1,128)} %param.8) | copy-start | bytes 1540
  483.6 44.5 %copy-start = (f32[512,512]{1,0:T(8,128)}, f32[512,512]{1,0:T(8,128)S(1)}, u32[]{:S(2)}) copy-start(f32[512,512]{1,0:T(8,128)S(1)} %fusion.6) | copy-start | bytes 3145732
  528.5 117.8 %slice-start = ((s8[6291456]{0:T(1024)(128)(4,1)}), s8[2097152]{0:T(1024)(128)(4,1)S(1)}, s32[]{:S(2)}) async-start(s8[6291456]{0:T(1024)(128)(4,1)} %bitcast.113), calls=%async_computation.3 | async-start | bytes 4194304
  580.2 66.1 %copy-start.1 = (f32[6144]{0:T(1024)S(1)}, f32[6144]{0:T(1024)}, u32[]{:S(2)}) copy-start(f32[6144]{0:T(1024)} %multiply_bitcast_fusion) | copy-start | bytes 73732
  638.6 7.7 %slice-start.1 = ((s8[6291456]{0:T(1024)(128)(4,1)}), s8[4194304]{0:T(1024)(128)(4,1)S(1)}, s32[]{:S(2)}) async-start(s8[6291456]{0:T(1024)(128)(4,1)} %bitcast.113), calls=%async_computation.4 | async-start | bytes 8388608
Sparse Core Ops, SparseCore 0:
  212.8 267.5 all-reduce.2
where the time goes:
time: 773 us; the launch traced here: 763 us
  waiting for transfers between devices  249 us (32%)
  blocking collectives  170 us (22%)
  local copies, waits for them, and re-layouts  158 us (20%)
  other arithmetic  136 us (18%)
  matrix products  23.9 us (3%)
  between operations  17.1 us (2%)
  starting transfers between devices  8.8 us (1%)
    psum x1, waiting for transfers between devices, reduce_gram(): lax.psum((gram_local, drive_local), ('member', 'grid'))  174 us
    unnamed x19, local copies, waits for them, and re-layouts  90.5 us
    psum x1, blocking collectives, reduce_gram(): lax.psum((gram_local, drive_local), ('member', 'grid'))  88.8 us
    another operation x15, other arithmetic, transform_matrix(): factor_low = jnp.linalg.cholesky(system)  85.3 us
    all_to_all x1, blocking collectives, local(): lax.all_to_all(updated, 'member', split_axis=0, concat_axis=2, tiled=True)  81.4 us
    all_to_all x1, waiting for transfers between devices, local(): lax.all_to_all(prior_ensemble, 'member', split_axis=2, concat_axis=0, til...  74.8 us
    another operation x3, other arithmetic, transform_matrix(): jax.scipy.linalg.solve_triangular(factor_low, identity, lower=True)  41.8 us
    all_to_all x1, local copies, waits for them, and re-layouts, local(): lax.all_to_all(prior_ensemble, 'member', split_axis=2, concat_axis=0, til...  18.8 us
  transfers between devices with their start and end apart: 2, of which 2 were waited for; matrix products, arithmetic and copies ran while one was open for 1% of the time, Pallas kernels for 0%

commit v1 on v0

--- a/solution.py
+++ b/solution.py
@@ -38,7 +38,7 @@
 
 def reduce_gram(whitened, innovation):
     gram_local, drive_local = local_sums(whitened, innovation)
-    gram_total, drive_vector = lax.psum((gram_local, drive_local), ("member", "grid"))
+    gram_total, drive_vector = lax.psum(lax.psum((gram_local, drive_local), "grid"), "member")
     return transform_matrix(gram_total, drive_vector)
 
 

time: 773 us -> 705 us (0.912)
  waiting for transfers between devices: 249 us -> 183 us
    psum x1 -> x2, waiting for transfers between devices: 174 us -> 106 us  [the longest x1 106 us: reduce_gram(): lax.psum(lax.psum((gram_local, drive_local), 'grid'), 'member')]
    psum x1 -> x2, blocking collectives: 88.8 us -> 89.8 us  [the longest x1 73.6 us: reduce_gram(): lax.psum(lax.psum((gram_local, drive_local), 'grid'), 'member')]
  transfers between devices with their start and end apart: 2 -> 3, of which waited for: 2 -> 2; matrix products, arithmetic and copies ran while one was open for 1% -> 1% of each run, Pallas kernels for 0% -> 0%
where the time goes in v1:
time: 705 us; the launch traced here: 696 us
  waiting for transfers between devices  183 us (26%)
  blocking collectives  169 us (24%)
  local copies, waits for them, and re-layouts  158 us (22%)
  other arithmetic  136 us (19%)
  matrix products  23.8 us (3%)
  between operations  17.1 us (2%)
  starting transfers between devices  8.84 us (1%)
    psum x1, waiting for transfers between devices, reduce_gram(): lax.psum(lax.psum((gram_local, drive_local), 'grid'), 'member')  106 us
    unnamed x19, local copies, waits for them, and re-layouts  90.5 us
    another operation x15, other arithmetic, transform_matrix(): factor_low = jnp.linalg.cholesky(system)  85.2 us
    all_to_all x1, blocking collectives, local(): lax.all_to_all(updated, 'member', split_axis=0, concat_axis=2, tiled=True)  79 us
    all_to_all x1, waiting for transfers between devices, local(): lax.all_to_all(prior_ensemble, 'member', split_axis=2, concat_axis=0, til...  76.5 us
    psum x1, blocking collectives, reduce_gram(): lax.psum(lax.psum((gram_local, drive_local), 'grid'), 'member')  73.6 us
    another operation x3, other arithmetic, transform_matrix(): jax.scipy.linalg.solve_triangular(factor_low, identity, lower=True)  41.9 us
    all_to_all x1, local copies, waits for them, and re-layouts, local(): lax.all_to_all(prior_ensemble, 'member', split_axis=2, concat_axis=0, til...  18.8 us
  transfers between devices with their start and end apart: 3, of which 2 were waited for; matrix products, arithmetic and copies ran while one was open for 1% of the time, Pallas kernels for 0%

profile of v1, /device:TPU:1, one launch (start us, length us, event | category | flops | bytes accessed | tf_op | source)
XLA Modules:
  0.0 695.5 jit_solution(6034240774330629529)
XLA Ops:
  6.5 19.4 %copy.19 = bf16[16,48,4096]{1,0,2:T(8,128)(2,1)} copy(bf16[16,48,4096]{2,1,0:T(8,128)(2,1)} %param.5) | data formatting | bytes 12582912 | tf_op args[0]
  25.9 31.8 %reshape.139 = bf16[32,2,49152]{2,1,0:T(2,128)(2,1)} reshape(bf16[4096,16,48]{2,1,0:T(8,128)(2,1)} %bitcast.111) | data formatting | bytes 12582912
  57.7 8.8 %all-to-all-start = ((bf16[32,2,49152]{2,1,0:T(2,128)(2,1)}), bf16[32,2,49152]{2,1,0:T(2,128)(2,1)}, u32[]{:S(2)}, u32[]{:S(2)}) async-start(bf16[32,2,49152]{2,1,0:T(2,128)(2,1)} %reshape.139), calls=%async_computation | async-start | bytes 12582912 | tf_op jit(solution)/shard_map/all_to_all | solution.py:62
  67.2 76.5 %all-to-all-done = bf16[32,2,49152]{2,1,0:T(2,128)(2,1)} async-done(((bf16[32,2,49152]{2,1,0:T(2,128)(2,1)}), bf16[32,2,49152]{2,1,0:T(2,128)(2,1)}, u32[]{:S(2)}, u32[]{:S(2)}) %all-to-all-start) | async-done | bytes 6291488 | tf_op jit(solution)/shard_map/all_to_all | solution.py:62
  143.7 27.6 %reshape.140 = bf16[4096,16,48]{2,1,0:T(8,128)(2,1)} reshape(bf16[32,2,49152]{2,1,0:T(2,128)(2,1)} %all-to-all-done) | data formatting | bytes 12582912
  171.3 18.8 %copy.20 = bf16[16,48,32,128]{3,1,0,2:T(8,128)(2,1)} copy(bf16[16,48,32,128]{1,0,3,2:T(8,128)(2,1)} %bitcast.110) | data formatting | bytes 12582912 | tf_op jit(solution)/shard_map/all_to_all | solution.py:62
  190.1 7.1 %copy.44 = bf16[64,8,48,128]{3,1,2,0:T(8,128)(2,1)} copy(bf16[64,8,48,128]{3,2,1,0:T(8,128)(2,1)} %bitcast.112) | data formatting | bytes 12582912
  197.1 8.7 %copy.21 = bf16[512,6144]{0,1:T(8,128)(2,1)} copy(bf16[512,6144]{1,0:T(8,128)(2,1)} %bitcast.119) | data formatting | bytes 12582912 | tf_op jit(solution)/shard_map/reshape | solution.py:47
  214.8 16.2 %psum.30 = f32[512]{0:T(512)S(1)} all-reduce(f32[512]{0:T(512)S(1)} %bitcast.121), channel_id=1, replica_groups=mesh['member'=32,'grid'=8] {'grid'}, use_global_device_ids=true, to_apply=%region_12.13 | all-reduce | flops 512 | bytes 4096 | tf_op jit(solution)/shard_map/psum | solution.py:41
  231.1 73.6 %psum.31 = f32[512]{0:T(512)S(1)} all-reduce(f32[512]{0:T(512)S(1)} %psum.30), channel_id=1, replica_groups=mesh['member'=32,'grid'=8] {'member'}, use_global_device_ids=true, to_apply=%region_13.14 | all-reduce | flops 512 | bytes 4096 | tf_op jit(solution)/shard_map/psum | solution.py:41
  309.4 106.3 %all-reduce.6.cloned.1.call-done = f32[512,512]{0,1:T(8,128)} async-done(((f32[512,512]{0,1:T(8,128)}), f32[512,512]{0,1:T(8,128)}) %all-reduce.6.cloned.1.call-update) | async-done | bytes 1048592 | tf_op jit(solution)/shard_map/psum | solution.py:41
  418.9 11.7 %cholesky.107 = f32[128,128]{1,0:T(8,128)S(1)} custom-call(f32[128,128]{1,0:T(8,128)S(1)} %cholesky.269), custom_call_target="Cholesky" | custom-call | tf_op jit(solution)/shard_map/jit(cholesky)/cholesky | solution.py:23
  430.6 9.8 %custom-call.31 = f32[1,128,128]{1,2,0:T(8,128)S(1)} custom-call(f32[1,128,128]{2,1,0:T(8,128)S(1)} %get-tuple-element.36), custom_call_target="InvertDiagBlocksLowerTriangular" | custom-call | tf_op jit(solution)/shard_map/jit(cholesky)/cholesky | solution.py:23
  441.1 11.9 %cholesky.221 = f32[128,128]{1,0:T(8,128)S(1)} custom-call(f32[128,128]{1,0:T(8,128)S(1)} %cholesky.273), custom_call_target="Cholesky" | custom-call | tf_op jit(solution)/shard_map/jit(cholesky)/cholesky | solution.py:23
  453.4 9.8 %custom-call.32 = f32[1,128,128]{1,2,0:T(8,128)S(1)} custom-call(f32[1,128,128]{2,1,0:T(8,128)S(1)} %get-tuple-element.34), custom_call_target="InvertDiagBlocksLowerTriangular" | custom-call | tf_op jit(solution)/shard_map/jit(cholesky)/cholesky | solution.py:23
  466.0 13.2 %cholesky.242 = f32[128,128]{1,0:T(8,128)} custom-call(f32[128,128]{1,0:T(8,128)} %cholesky.278), custom_call_target="Cholesky" | custom-call | tf_op jit(solution)/shard_map/jit(cholesky)/cholesky | solution.py:23
  483.0 11.3 %custom-call.33 = f32[1,128,128]{1,2,0:T(8,128)} custom-call(f32[1,128,128]{2,1,0:T(8,128)} %get-tuple-element.32), custom_call_target="InvertDiagBlocksLowerTriangular" | custom-call | tf_op jit(solution)/shard_map/jit(cholesky)/cholesky | solution.py:23
  496.8 12.1 %cholesky.259 = f32[128,128]{1,0:T(8,128)S(1)} custom-call(f32[128,128]{1,0:T(8,128)S(1)} %convolution_subtract_fusion.5), custom_call_target="Cholesky" | custom-call | tf_op jit(solution)/shard_map/jit(cholesky)/cholesky | solution.py:23
  517.2 14.2 %while.1 = (s32[]{:T(128)}, f32[512,512]{0,1:T(8,128)}, s32[4,2]{0,1:T(2,128)S(1)}, f32[4,128,128]{2,1,0:T(8,128)}, s32[]{:T(128)}) while((s32[]{:T(128)}, f32[512,512]{0,1:T(8,128)}, s32[4,2]{0,1:T(2,128)S(1)}, f32[4,128,128]{2,1,0:T(8,128)}, s32[]{:T(128)}) %tuple.25), condition=%wide.while_cond, body=%wide.while_body.sunk | while | flops 2 | bytes 393829 | solution.py:24
  531.4 40.1 %custom-call.34 = f32[4,128,128]{1,2,0:T(8,128)S(1)} custom-call(f32[4,128,128]{2,1,0:T(8,128)} %get-tuple-element.12), custom_call_target="InvertDiagBlocksLowerTriangular" | custom-call | tf_op jit(solution)/shard_map/jit(_solve_triangular)/triangular_solve | solution.py:24
  581.2 6.7 fusion.1
  592.6 79.0 %all_to_all.33 = bf16[512,48,128]{2,1,0:T(8,128)(2,1)S(1)} all-to-all(bf16[512,48,128]{2,1,0:T(8,128)(2,1)S(1)} %bitcast.116), channel_id=1, replica_groups=mesh['member'=32,'grid'=8] {'member'}, dimensions={0} | all-to-all | bytes 12582912 | tf_op jit(solution)/shard_map/all_to_all | solution.py:72
  671.5 6.7 copy.45
  678.2 10.3 %all_to_all.30 = bf16[16,48,4096]{2,1,0:T(8,128)(2,1)} reshape(bf16[16,48,32,128]{3,2,1,0:T(8,128)(2,1)} %bitcast.118) | data formatting | bytes 12582912 | tf_op jit(solution)/shard_map/all_to_all | solution.py:72
  (96 shorter events, 61.3 us)
Async XLA Ops:
  57.6 9.5 %copy-start.3 = (s32[1,1,128]{2,1,0:T(1,128)S(1)}, s32[1,1,128]{2,1,0:T(1,128)}, u32[]{:S(2)}) copy-start(s32[1,1,128]{2,1,0:T(1,128)} %param.6) | copy-start | bytes 1540
  57.7 86.1 %all-to-all-start = ((bf16[32,2,49152]{2,1,0:T(2,128)(2,1)}), bf16[32,2,49152]{2,1,0:T(2,128)(2,1)}, u32[]{:S(2)}, u32[]{:S(2)}) async-start(bf16[32,2,49152]{2,1,0:T(2,128)(2,1)} %reshape.139), calls=%async_computation | async-start | bytes 12582912 | tf_op jit(solution)/shard_map/all_to_all | solution.py:62
  66.4 238.3 %all-reduce.4.cloned.1.call-start = ((), (), s32[]{:S(2)}) async-start(), calls=%async_computation.2 | async-start | bytes 2097152 | tf_op jit(solution)/shard_map/psum | solution.py:41
  197.1 13.3 %copy-start.2 = (f32[1,1,128]{2,1,0:T(1,128)S(1)}, f32[1,1,128]{2,1,0:T(1,128)}, u32[]{:S(2)}) copy-start(f32[1,1,128]{2,1,0:T(1,128)} %param.9) | copy-start | bytes 1540
  197.1 17.4 %copy-start.4 = (f32[1,1,128]{2,1,0:T(1,128)S(1)}, f32[1,1,128]{2,1,0:T(1,128)}, u32[]{:S(2)}) copy-start(f32[1,1,128]{2,1,0:T(1,128)} %param.8) | copy-start | bytes 1540
  212.7 203.1 %all-reduce.6.cloned.1.call-start = ((), (), s32[]{:S(2)}) async-start(), calls=%async_computation.3 | async-start | bytes 2097152 | tf_op jit(solution)/shard_map/psum | solution.py:41
  418.9 44.5 %copy-start = (f32[512,512]{1,0:T(8,128)}, f32[512,512]{1,0:T(8,128)S(1)}, u32[]{:S(2)}) copy-start(f32[512,512]{1,0:T(8,128)S(1)} %fusion.6) | copy-start | bytes 3145732
  463.7 117.5 %slice-start = ((s8[6291456]{0:T(1024)(128)(4,1)}), s8[2097152]{0:T(1024)(128)(4,1)S(1)}, s32[]{:S(2)}) async-start(s8[6291456]{0:T(1024)(128)(4,1)} %bitcast.113), calls=%async_computation.4 | async-start | bytes 4194304
  515.3 65.8 %copy-start.1 = (f32[6144]{0:T(1024)S(1)}, f32[6144]{0:T(1024)}, u32[]{:S(2)}) copy-start(f32[6144]{0:T(1024)} %multiply_bitcast_fusion) | copy-start | bytes 73732
  573.5 7.7 %slice-start.1 = ((s8[6291456]{0:T(1024)(128)(4,1)}), s8[4194304]{0:T(1024)(128)(4,1)S(1)}, s32[]{:S(2)}) async-start(s8[6291456]{0:T(1024)(128)(4,1)} %bitcast.113), calls=%async_computation.5 | async-start | bytes 8388608
Sparse Core Ops, SparseCore 0:
  212.8 81.4 all-reduce.3
  304.8 110.8 all-reduce.5
